TPU v7x, 32 devices: a whole 2x2x4 slice. The times are simulated.
32 devices in a mesh: row: 4 (over z), col: 8 (over y, x, core).
Axes of the slice: x: 2, y: 2, z: 4, core: 2. Of those that a mesh axis runs over, the one named last changes fastest.
Arguments:
- features: bfloat16 [8, 1024, 256], P('col', 'row'), may hold values from -6 to 6
- weight: bfloat16 [256, 256], replicated, may hold values from -0.375 to 0.375
- cotangent: bfloat16 [8192, 256], P(('row', 'col')), may hold values from -6 to 6
- blk_vals: bfloat16 [4, 8, 192, 128, 128], P('row', 'col'), may hold values from -0.0546875 to 0.0546875
- blk_rows: int32 [4, 8, 192], P('row', 'col'), may hold values from 0 to 15
- blk_cols: int32 [4, 8, 192], P('row', 'col'), may hold values from 0 to 7
- blk_count: int32 [4, 8], P('row', 'col'), may hold values from 24 to 192, as said below
Outputs:
- activated: bfloat16 [8192, 256], P(('row', 'col'))
- grad_weight: float32 [256, 256], replicated
- grad_features: bfloat16 [8, 1024, 256], P('col', 'row')
Inputs may be any that keep to these rules, and one draw needn't show every extreme that they name: Only the first blk_count slots of a panel pair are used; a pair whose row and column node ranges intersect uses all 192, every other pair at most 96.
All inputs are finite; a program needn't handle non-finite values.
Results may differ from a plain program's by a relative error of at most 0.0059.
Values may be sent and summed in bfloat16 or wider, within the bound.
A program may use at most 128 MiB of HBM per device.

v0:
```python
import jax
import jax.numpy as jnp
from jax import lax
from jax.sharding import PartitionSpec as P


def block_terms(values, index, source, live_count, transpose):
    total_slots = values.shape[0]
    group = 64
    width = source.shape[-1]
    side = values.shape[-1]
    if transpose:
        form = "bji,bjf->bif"
    else:
        form = "bij,bjf->bif"

    def one_group(group_index, buffer):
        first = group_index * group
        block_vals = lax.dynamic_slice_in_dim(values, first, group, 0)
        block_ids = lax.dynamic_slice_in_dim(index, first, group, 0)
        picked = jnp.take(source, block_ids, axis=0)
        product = jnp.einsum(form, block_vals, picked, preferred_element_type=jnp.float32)
        alive = first + jnp.arange(group, dtype=jnp.int32) < live_count
        product = jnp.where(alive[:, None, None], product, 0.0)
        return lax.dynamic_update_slice_in_dim(buffer, product, first, 0)

    buffer = jnp.zeros((total_slots, side, width), jnp.float32)
    groups = total_slots // group
    return lax.fori_loop(0, groups, one_group, buffer)


def per_device(features, weight, cotangent, blk_vals, blk_rows, blk_cols, blk_count):
    rows_here = cotangent.shape[0]
    width = cotangent.shape[1]
    side = blk_vals.shape[-1]
    row_blocks = rows_here * lax.axis_size("col") // side
    col_blocks = rows_here * lax.axis_size("row") // side
    values = blk_vals[0, 0]
    row_ids = blk_rows[0, 0]
    col_ids = blk_cols[0, 0]
    live_count = blk_count[0, 0]
    panel = lax.all_gather(features, "row", axis=1, tiled=True)
    source = panel.reshape(col_blocks, side, width)
    products = block_terms(values, col_ids, source, live_count, False)
    partial_rows = jax.ops.segment_sum(products, row_ids, num_segments=row_blocks)
    own_rows = lax.psum_scatter(
        partial_rows.reshape(row_blocks * side, width), "col", scatter_dimension=0, tiled=True
    )
    aggregated = own_rows.astype(jnp.bfloat16)
    pre = jnp.dot(aggregated, weight, preferred_element_type=jnp.float32)
    sigma = jax.nn.sigmoid(pre)
    activated = (pre * sigma).astype(jnp.bfloat16)
    grad_pre = (cotangent.astype(jnp.float32) * sigma * (1.0 + pre * (1.0 - sigma))).astype(
        jnp.bfloat16
    )
    local_weight = lax.dot_general(
        aggregated, grad_pre, (((0,), (0,)), ((), ())), preferred_element_type=jnp.float32
    )
    grad_weight = lax.psum(local_weight, ("row", "col"))
    grad_agg = lax.dot_general(
        grad_pre, weight, (((1,), (1,)), ((), ())), preferred_element_type=jnp.float32
    ).astype(jnp.bfloat16)
    grad_rows = lax.all_gather(grad_agg, "col", axis=0, tiled=True)
    grad_source = grad_rows.reshape(row_blocks, side, width)
    back_products = block_terms(values, row_ids, grad_source, live_count, True)
    partial_cols = jax.ops.segment_sum(back_products, col_ids, num_segments=col_blocks)
    own_cols = lax.psum_scatter(
        partial_cols.reshape(col_blocks * side, width), "row", scatter_dimension=0, tiled=True
    )
    grad_features = own_cols.astype(jnp.bfloat16).reshape(1, rows_here, width)
    return (activated, grad_weight, grad_features)


def solution(mesh):
    return jax.shard_map(
        per_device,
        mesh=mesh,
        in_specs=(
            P("col", "row", None),
            P(),
            P(("row", "col"), None),
            P("row", "col", None, None, None),
            P("row", "col", None),
            P("row", "col", None),
            P("row", "col"),
        ),
        out_specs=(P(("row", "col"), None), P(), P("col", "row", None)),
        check_vma=False,
    )
```

profile of v0, /device:TPU:0, one launch (start us, length us, event | category | flops | bytes accessed | tf_op | source)
XLA Modules:
  0.0 424.0 jit_solution(15833494370647342353)
XLA Ops:
  7.2 17.6 %all_gather.6 = bf16[1,1024,256]{2,1,0:T(8,128)(2,1)S(1)} all-gather(bf16[1,256,256]{2,1,0:T(8,128)(2,1)} %param.11), channel_id=1, replica_groups=mesh['row'=4,'col'=8] {'row'}, dimensions={1}, use_global_device_ids=true | all-gather | bytes 655360 | tf_op jit(solution)/shard_map/all_gather | solution.py:42
  24.8 11.5 %broadcast.44.clone = f32[192,128,256]{2,1,0:T(8,128)} broadcast(f32[]{:T(128)} %constant.131.clone.1), dimensions={} | broadcast | bytes 25165828 | tf_op jit(solution)/shard_map/broadcast.3
  36.3 32.7 %while.26 = (s32[]{:T(128)}, f32[192,128,256]{2,1,0:T(8,128)}, s32[]{:T(128)}, bf16[192,128,128]{2,1,0:T(8,128)(2,1)}, s32[192]{0:T(256)S(1)}, /*index=5*/bf16[8...) while((s32[]{:T(128)}, f32[192,128,256]{2,1,0:T(8,128)}, s32[]{:T(128)}, ...), condition=%wide.region_1.0_spmd, body=%wide.region_0.1_spmd.sunk | while | flops 541066752 | bytes 23075232 | solution.py:29
  37.1 2.8 gather_fusion
  39.8 7.4 %select_dynamic-update-slice_fusion.4 = f32[192,128,256]{2,1,0:T(8,128)} fusion(f32[192,128,256]{2,1,0:T(8,128)} %get-tuple-element.358, s32[]{:T(128)S(6)} %select_n.88, pred[64]{0:T(512)(128)(4,1)S(1)} %get-tuple-element.335, bf16[64,128,256]{2,1,0:T(8,128)(2,1)} %gather_fusion, pred[64]{0:T(512)(128)(4,1)S(1)} %get-tuple-element.337, ...), kind=kOutput, calls=%fused_computation.4.clone.1 | convolution fusion | flops 541065216 | bytes 14681216 | tf_op jit(solution)/shard_map/while/body/eval_jaxpr/bij,bjf->bif/dot_general | solution.py:22
  47.9 2.8 gather_fusion
  50.7 7.4 %select_dynamic-update-slice_fusion.4 = f32[192,128,256]{2,1,0:T(8,128)} fusion(f32[192,128,256]{2,1,0:T(8,128)} %get-tuple-element.358, s32[]{:T(128)S(6)} %select_n.88, pred[64]{0:T(512)(128)(4,1)S(1)} %get-tuple-element.335, bf16[64,128,256]{2,1,0:T(8,128)(2,1)} %gather_fusion, pred[64]{0:T(512)(128)(4,1)S(1)} %get-tuple-element.337, ...), kind=kOutput, calls=%fused_computation.4.clone.1 | convolution fusion | flops 541065216 | bytes 14681216 | tf_op jit(solution)/shard_map/while/body/eval_jaxpr/bij,bjf->bif/dot_general | solution.py:22
  58.8 2.8 gather_fusion
  61.6 7.4 %select_dynamic-update-slice_fusion.4 = f32[192,128,256]{2,1,0:T(8,128)} fusion(f32[192,128,256]{2,1,0:T(8,128)} %get-tuple-element.358, s32[]{:T(128)S(6)} %select_n.88, pred[64]{0:T(512)(128)(4,1)S(1)} %get-tuple-element.335, bf16[64,128,256]{2,1,0:T(8,128)(2,1)} %gather_fusion, pred[64]{0:T(512)(128)(4,1)S(1)} %get-tuple-element.337, ...), kind=kOutput, calls=%fused_computation.4.clone.1 | convolution fusion | flops 541065216 | bytes 14681216 | tf_op jit(solution)/shard_map/while/body/eval_jaxpr/bij,bjf->bif/dot_general | solution.py:22
  69.2 36.1 %scatter_fusion = f32[16,128,256]{2,1,0:T(8,128)S(1)} fusion(f32[16,128,256]{2,1,0:T(8,128)S(1)} %broadcast_in_dim.108, s32[192]{0:T(256)S(1)} %bitcast.22, f32[192,128,256]{2,1,0:T(8,128)} %get-tuple-element.221), kind=kCustom, calls=%fused_computation.2 | custom fusion | flops 6291456 | bytes 75498240 | tf_op jit(solution)/shard_map/scatter-add | solution.py:45
  106.7 43.0 %reduce-scatter.3.cloned.1.call-done = f32[256,256]{1,0:T(8,128)} async-done(((f32[2048,256]{1,0:T(8,128)}), f32[256,256]{1,0:T(8,128)}) %reduce-scatter.3.cloned.1.call-update) | async-done | bytes 262160 | tf_op jit(solution)/shard_map/reduce_scatter | solution.py:46
  152.6 8.6 %copy.10 = bf16[1,1,192,128,128]{3,4,2,1,0:T(8,128)(2,1)} copy(bf16[1,1,192,128,128]{4,3,2,1,0:T(8,128)(2,1)} %bitcast.20) | data formatting | bytes 12582912 | tf_op args[3]
  161.1 14.9 %all-gather.2.cloned.1.call-done = bf16[2048,256]{1,0:T(8,128)(2,1)} async-done(((bf16[256,256]{1,0:T(8,128)(2,1)}), bf16[2048,256]{1,0:T(8,128)(2,1)}) %all-gather.2.cloned.1.call-update) | async-done | bytes 1048592 | tf_op jit(solution)/shard_map/all_gather | solution.py:63
  176.0 11.5 %broadcast.44 = f32[192,128,256]{2,1,0:T(8,128)} broadcast(f32[]{:T(128)} %constant.131.clone.1), dimensions={} | broadcast | bytes 25165828 | tf_op jit(solution)/shard_map/broadcast.3
  187.5 32.7 %while.27 = (s32[]{:T(128)}, f32[192,128,256]{2,1,0:T(8,128)}, s32[]{:T(128)}, bf16[192,128,128]{1,2,0:T(8,128)(2,1)}, s32[192]{0:T(256)S(1)}, /*index=5*/bf16[1...) while((s32[]{:T(128)}, f32[192,128,256]{2,1,0:T(8,128)}, s32[]{:T(128)}, ...), condition=%wide.region_6.7_spmd, body=%wide.region_5.6_spmd.sunk | while | flops 541066752 | bytes 23075232 | solution.py:29
  188.3 2.8 gather_fusion.1
  191.0 7.4 %select_dynamic-update-slice_fusion.5 = f32[192,128,256]{2,1,0:T(8,128)} fusion(f32[192,128,256]{2,1,0:T(8,128)} %get-tuple-element.388, s32[]{:T(128)S(6)} %select_n.91, pred[64]{0:T(512)(128)(4,1)S(1)} %get-tuple-element.344, bf16[64,128,256]{2,1,0:T(8,128)(2,1)} %gather_fusion.1, pred[64]{0:T(512)(128)(4,1)S(1)} %get-tuple-element.346, ...), kind=kOutput, calls=%fused_computation.16.clone.1 | convolution fusion | flops 541065216 | bytes 14681216 | tf_op jit(solution)/shard_map/while/body/eval_jaxpr/bji,bjf->bif/dot_general | solution.py:22
  199.1 2.8 gather_fusion.1
  201.9 7.4 %select_dynamic-update-slice_fusion.5 = f32[192,128,256]{2,1,0:T(8,128)} fusion(f32[192,128,256]{2,1,0:T(8,128)} %get-tuple-element.388, s32[]{:T(128)S(6)} %select_n.91, pred[64]{0:T(512)(128)(4,1)S(1)} %get-tuple-element.344, bf16[64,128,256]{2,1,0:T(8,128)(2,1)} %gather_fusion.1, pred[64]{0:T(512)(128)(4,1)S(1)} %get-tuple-element.346, ...), kind=kOutput, calls=%fused_computation.16.clone.1 | convolution fusion | flops 541065216 | bytes 14681216 | tf_op jit(solution)/shard_map/while/body/eval_jaxpr/bji,bjf->bif/dot_general | solution.py:22
  210.0 2.8 gather_fusion.1
  212.8 7.4 %select_dynamic-update-slice_fusion.5 = f32[192,128,256]{2,1,0:T(8,128)} fusion(f32[192,128,256]{2,1,0:T(8,128)} %get-tuple-element.388, s32[]{:T(128)S(6)} %select_n.91, pred[64]{0:T(512)(128)(4,1)S(1)} %get-tuple-element.344, bf16[64,128,256]{2,1,0:T(8,128)(2,1)} %gather_fusion.1, pred[64]{0:T(512)(128)(4,1)S(1)} %get-tuple-element.346, ...), kind=kOutput, calls=%fused_computation.16.clone.1 | convolution fusion | flops 541065216 | bytes 14681216 | tf_op jit(solution)/shard_map/while/body/eval_jaxpr/bji,bjf->bif/dot_general | solution.py:22
  220.3 36.0 %scatter_fusion.1 = f32[8,128,256]{2,1,0:T(8,128)S(1)} fusion(f32[8,128,256]{2,1,0:T(8,128)S(1)} %broadcast_in_dim.109, s32[192]{0:T(256)S(1)} %get-tuple-element.427, f32[192,128,256]{2,1,0:T(8,128)} %get-tuple-element.222), kind=kCustom, calls=%fused_computation.3 | custom fusion | flops 6291456 | bytes 75498240 | tf_op jit(solution)/shard_map/scatter-add | solution.py:66
  258.3 26.4 %reduce-scatter.5.cloned.1.call-done = f32[256,256]{1,0:T(8,128)} async-done(((f32[1024,256]{1,0:T(8,128)}), f32[256,256]{1,0:T(8,128)}) %reduce-scatter.5.cloned.1.call-update) | async-done | bytes 262160 | tf_op jit(solution)/shard_map/reduce_scatter | solution.py:67
  286.4 129.4 %all-reduce.2.cloned.1.call-done = f32[256,256]{1,0:T(8,128)} async-done(((f32[256,256]{1,0:T(8,128)}), f32[256,256]{1,0:T(8,128)}) %all-reduce.2.cloned.1.call-update) | async-done | bytes 262160 | tf_op jit(solution)/shard_map/psum | solution.py:59
  (45 shorter events, 14.2 us)
Async XLA Ops:
  7.2 142.5 %copy-start = (bf16[256,256]{1,0:T(8,128)(2,1)S(1)}, bf16[256,256]{1,0:T(8,128)(2,1)}, u32[]{:S(2)}) copy-start(bf16[256,256]{1,0:T(8,128)(2,1)} %param.12) | copy-start | bytes 393220
  7.2 142.5 %reduce-scatter.3.cloned.1.call-start = ((), (), s32[]{:S(2)}) async-start(), calls=%async_computation.2 | async-start | bytes 2359296 | tf_op jit(solution)/shard_map/reduce_scatter | solution.py:46
  24.8 11.5 %copy-start.7 = (s32[1,1,192]{2,1,0:T(1,128)S(1)}, s32[1,1,192]{2,1,0:T(1,128)}, u32[]{:S(2)}) copy-start(s32[1,1,192]{2,1,0:T(1,128)} %param.16) | copy-start | bytes 2308
  36.3 32.9 %copy-start.6 = (s32[1,1,192]{2,1,0:T(1,128)S(1)}, s32[1,1,192]{2,1,0:T(1,128)}, u32[]{:S(2)}) copy-start(s32[1,1,192]{2,1,0:T(1,128)} %param.15) | copy-start | bytes 2308
  69.2 80.5 %copy-start.8 = (bf16[256,256]{1,0:T(8,128)(2,1)S(1)}, bf16[256,256]{1,0:T(8,128)(2,1)}, u32[]{:S(2)}) copy-start(bf16[256,256]{1,0:T(8,128)(2,1)} %param.13) | copy-start | bytes 393220
  105.3 1.3 copy-start.4
  106.7 69.4 %all-gather.2.cloned.1.call-start = ((), (), s32[]{:S(2)}) async-start(), calls=%async_computation.4 | async-start | bytes 1179648 | tf_op jit(solution)/shard_map/all_gather | solution.py:63
  152.5 132.2 %reduce-scatter.5.cloned.1.call-start = ((), (), s32[]{:S(2)}) async-start(), calls=%async_computation.5 | async-start | bytes 1310720 | tf_op jit(solution)/shard_map/reduce_scatter | solution.py:67
  176.0 11.5 %copy-start.3 = (bf16[2048,256]{1,0:T(8,128)(2,1)S(1)}, bf16[2048,256]{1,0:T(8,128)(2,1)}, u32[]{:S(2)}) copy-start(bf16[2048,256]{1,0:T(8,128)(2,1)} %all-gather.2.cloned.1.call-done) | copy-start | bytes 3145732
  220.3 37.1 %copy-start.5 = (f32[256,256]{1,0:T(8,128)S(1)}, f32[256,256]{1,0:T(8,128)}, u32[]{:S(2)}) copy-start(f32[256,256]{1,0:T(8,128)} %reduce-scatter.3.cloned.1.call-done) | copy-start | bytes 786436
  220.3 197.2 %copy-start.1 = (bf16[256,256]{1,0:T(8,128)(2,1)S(1)}, bf16[256,256]{1,0:T(8,128)(2,1)}, u32[]{:S(2)}) copy-start(bf16[256,256]{1,0:T(8,128)(2,1)} %param.12) | copy-start | bytes 393220
  256.3 1.0 copy-start.2
  257.3 158.5 %all-reduce.2.cloned.1.call-start = ((), (), s32[]{:S(2)}) async-start(), calls=%async_computation.3 | async-start | bytes 524288 | tf_op jit(solution)/shard_map/psum | solution.py:59
Sparse Core Ops, SparseCore 0:
  106.8 42.8 reduce-scatter.2
  152.6 23.3 all-gather.1
  257.4 27.2 reduce-scatter.4
  290.7 125.0 all-reduce.1
where the time goes:
time: 425 us; the launch traced here: 424 us
  waiting for transfers between devices  214 us (50%)
  other arithmetic  78.1 us (18%)
  local copies, waits for them, and re-layouts  52.5 us (12%)
  matrix products  47.9 us (11%)
  blocking collectives  17.6 us (4%)
  between operations  13.9 us (3%)
    psum x1, waiting for transfers between devices, per_device(): grad_weight = lax.psum(local_weight, ('row', 'col'))  129 us
    dot_general x6, matrix products, one_group(): jnp.einsum(form, block_vals, picked, preferred_element_type=jnp.float32)  44.3 us
    reduce_scatter x1, waiting for transfers between devices, per_device(): lax.psum_scatter(partial_rows.reshape(row_blocks * side, width), 'col', s...  43 us
    scatter-add x1, other arithmetic, per_device(): jax.ops.segment_sum(products, row_ids, num_segments=row_blocks)  36.1 us
    scatter-add x1, other arithmetic, per_device(): jax.ops.segment_sum(back_products, col_ids, num_segments=col_blocks)  36 us
    reduce_scatter x1, waiting for transfers between devices, per_device(): lax.psum_scatter(partial_cols.reshape(col_blocks * side, width), 'row', s...  26.4 us
    another operation x2, local copies, waits for them, and re-layouts  23 us
    all_gather x1, blocking collectives, per_device(): panel = lax.all_gather(features, 'row', axis=1, tiled=True)  17.6 us
  transfers between devices with their start and end apart: 4, of which 4 were waited for; matrix products, arithmetic and copies ran while one was open for 3% of the time, Pallas kernels for 0%

commit v1 on v0

--- a/solution.py
+++ b/solution.py
@@ -1,7 +1,16 @@
+import functools
+
 import jax
 import jax.numpy as jnp
 from jax import lax
+from jax.experimental import pallas as pl
+from jax.experimental.pallas import tpu as pltpu
 from jax.sharding import PartitionSpec as P
+
+MESH = pl.DeviceIdType.MESH
+F32 = jnp.float32
+BF16 = jnp.bfloat16
+DENSE_LIMIT = 16 * 1024 * 1024
 
 
 def block_terms(values, index, source, live_count, transpose):
@@ -29,7 +38,7 @@
     return lax.fori_loop(0, groups, one_group, buffer)
 
 
-def per_device(features, weight, cotangent, blk_vals, blk_rows, blk_cols, blk_count):
+def blockwise_device(features, weight, cotangent, blk_vals, blk_rows, blk_cols, blk_count):
     rows_here = cotangent.shape[0]
     width = cotangent.shape[1]
     side = blk_vals.shape[-1]
@@ -71,6 +80,313 @@
     return (activated, grad_weight, grad_features)
 
 
+def densify_kernel(cb, rows_ref, cols_ref, count_ref, vals_ref, out_ref, acc):
+    step = pl.program_id(0)
+    chunk, side = vals_ref.shape[0], vals_ref.shape[1]
+    cells = acc.shape[0]
+
+    @pl.when(step == 0)
+    def _():
+        def zero(i, carry):
+            acc[i] = jnp.zeros((side, side), F32)
+            return carry
+
+        lax.fori_loop(0, cells, zero, 0)
+
+    first = step * chunk
+    live = jnp.clip(count_ref[0] - first, 0, chunk)
+
+    def add(i, carry):
+        slot = first + i
+        cell = rows_ref[slot] * cb + cols_ref[slot]
+        acc[cell] = acc[cell] + vals_ref[i].astype(F32)
+        return carry
+
+    lax.fori_loop(0, live, add, 0)
+
+    @pl.when(step == pl.num_programs(0) - 1)
+    def _():
+        def put(i, carry):
+            for j in range(cb):
+                out_ref[pl.ds(pl.multiple_of(i * side, side), side), j * side : (j + 1) * side] = acc[
+                    i * cb + j
+                ].astype(BF16)
+            return carry
+
+        lax.fori_loop(0, cells // cb, put, 0)
+
+
+def densify(values, row_ids, col_ids, count, rb, cb):
+    slots, side = values.shape[0], values.shape[1]
+    chunk = 32
+    return pl.pallas_call(
+        functools.partial(densify_kernel, cb),
+        out_shape=jax.ShapeDtypeStruct((rb * side, cb * side), BF16),
+        grid_spec=pltpu.PrefetchScalarGridSpec(
+            num_scalar_prefetch=3,
+            grid=(slots // chunk,),
+            in_specs=[pl.BlockSpec((chunk, side, side), lambda i, *_: (i, 0, 0))],
+            out_specs=pl.BlockSpec((rb * side, cb * side), lambda i, *_: (0, 0)),
+            scratch_shapes=[pltpu.VMEM((rb * cb, side, side), F32)],
+        ),
+        name="densify",
+    )(row_ids, col_ids, count, values)
+
+
+def layer_kernel(
+    nr, nc,
+    x_ref, w_ref, ct_ref, a_hbm, act_ref, gw_ref, gf_ref,
+    a_ref, xs, pf, sib_out, sib_in, chip_out, chip_in, gbuf, qt, z_out, z_in,
+    lw, gw_in, gw_own, gw_row, gw_all,
+    a_sem, x_s, x_r, sib_s, sib_r, chip_s, chip_r, g_s, g_r, f_s, f_r, z_s, z_r,
+    w1_s, w1_r, w2_s, w2_r, w3_s, w3_r,
+):
+    r = lax.axis_index("row")
+    c = lax.axis_index("col")
+    nq = nc // 2
+    q = c // 2
+    core = c % 2
+    sib = 2 * q + (1 - core)
+    rd, width = x_ref.shape
+    wr = width // nc
+
+    def remote(src, dst, s, t, where):
+        return pltpu.make_async_remote_copy(
+            src_ref=src, dst_ref=dst, send_sem=s, recv_sem=t, device_id=where, device_id_type=MESH
+        )
+
+    load_a = pltpu.make_async_copy(a_hbm, a_ref, a_sem)
+    load_a.start()
+
+    barrier = pltpu.get_barrier_semaphore()
+    for j in range(1, nr):
+        pl.semaphore_signal(barrier, inc=1, device_id={"row": (r + j) % nr}, device_id_type=MESH)
+    for j in range(1, nc):
+        pl.semaphore_signal(barrier, inc=1, device_id={"col": (c + j) % nc}, device_id_type=MESH)
+    pl.semaphore_wait(barrier, nr + nc - 2)
+
+    def rows(i):
+        return pl.ds(pl.multiple_of(i * rd, rd), rd)
+
+    x_copies = [
+        remote(x_ref, xs.at[j - 1], x_s.at[j - 1], x_r.at[j - 1], {"row": (r + j) % nr})
+        for j in range(1, nr)
+    ]
+    for copy in x_copies:
+        copy.start()
+    load_a.wait()
+
+    def own_term(d, carry):
+        pf[d] = jnp.dot(a_ref[rows(d), rows(r)], x_ref[...], preferred_element_type=F32)
+        return carry
+
+    lax.fori_loop(0, nc, own_term, 0)
+    order = sorted(range(1, nr), key=lambda j: min(j, nr - j))
+    for j in order[:-1]:
+        x_copies[j - 1].wait_recv()
+
+        def add_term(d, carry, j=j):
+            pf[d] += jnp.dot(
+                a_ref[rows(d), rows((r + nr - j) % nr)], xs[j - 1], preferred_element_type=F32
+            )
+            return carry
+
+        lax.fori_loop(0, nc, add_term, 0)
+    last = order[-1]
+    x_copies[last - 1].wait_recv()
+
+    def total(d):
+        return pf[d] + jnp.dot(
+            a_ref[rows(d), rows((r + nr - last) % nr)], xs[last - 1], preferred_element_type=F32
+        )
+
+    sib_copies = []
+    for t in range(nq):
+        chip = (q + t + 1) % nq
+        sib_out[t] = total(2 * chip + (1 - core)).astype(BF16)
+        copy = remote(sib_out.at[t], sib_in.at[t], sib_s.at[t], sib_r.at[t], {"col": sib})
+        copy.start()
+        sib_copies.append(copy)
+    chip_copies = []
+    for t in range(nq):
+        d = 2 * ((q + t + 1) % nq) + core
+        value = total(d)
+        sib_copies[t].wait_recv()
+        value = value + sib_in[t].astype(F32)
+        if t < nq - 1:
+            chip_out[t] = value.astype(BF16)
+            copy = remote(chip_out.at[t], chip_in.at[t], chip_s.at[t], chip_r.at[t], {"col": d})
+            copy.start()
+            chip_copies.append(copy)
+        else:
+            pf[0] = value
+    agg = pf[0]
+    for t in range(nq - 1):
+        chip_copies[t].wait_recv()
+        agg = agg + chip_in[t].astype(F32)
+    agg = agg.astype(BF16)
+
+    pre = jnp.dot(agg, w_ref[...], preferred_element_type=F32)
+    sigma = jax.nn.sigmoid(pre)
+    act_ref[...] = (pre * sigma).astype(BF16)
+    grad_pre = (ct_ref[...].astype(F32) * sigma * (1.0 + pre * (1.0 - sigma))).astype(BF16)
+    gbuf[0, 0] = lax.dot_general(
+        w_ref[...], grad_pre, (((1,), (1,)), ((), ())), preferred_element_type=F32
+    ).astype(BF16)
+
+    g_copies = [
+        remote(gbuf.at[0, 0], gbuf.at[j, 0], g_s.at[j - 1], g_r.at[j - 1], {"col": 2 * ((q + j) % nq) + core})
+        for j in range(1, nq)
+    ]
+    f_copies = [
+        remote(gbuf.at[j, 0], gbuf.at[j, 1], f_s.at[j], f_r.at[j], {"col": sib}) for j in range(nq)
+    ]
+    for copy in g_copies:
+        copy.start()
+    f_copies[0].start()
+
+    lw[...] = lax.dot_general(agg, grad_pre, (((0,), (0,)), ((), ())), preferred_element_type=F32)
+    w1 = []
+    for j in range(1, nc):
+        d = (c + j) % nc
+        copy = remote(
+            lw.at[pl.ds(pl.multiple_of(d * wr, wr), wr), :], gw_in.at[j - 1],
+            w1_s.at[j - 1], w1_r.at[j - 1], {"col": d},
+        )
+        copy.start()
+        w1.append(copy)
+
+    def a_rows(j, e):
+        return rows(2 * ((q + nq - j) % nq) + (core if e == 0 else 1 - core))
+
+    qt[...] = jnp.dot(gbuf[0, 0], a_ref[a_rows(0, 0), :], preferred_element_type=F32)
+    for j in range(1, nq):
+        f_copies[j - 1].wait_recv()
+        qt[...] += jnp.dot(gbuf[j - 1, 1], a_ref[a_rows(j - 1, 1), :], preferred_element_type=F32)
+        g_copies[j - 1].wait_recv()
+        f_copies[j].start()
+        qt[...] += jnp.dot(gbuf[j, 0], a_ref[a_rows(j, 0), :], preferred_element_type=F32)
+
+    own_gw = lw[pl.ds(pl.multiple_of(c * wr, wr), wr), :]
+    for copy in w1:
+        copy.wait_recv()
+    for j in range(1, nc):
+        own_gw = own_gw + gw_in[j - 1]
+    gw_own[...] = own_gw
+    w2 = []
+    for j in range(1, nr):
+        copy = remote(gw_own, gw_row.at[j - 1], w2_s.at[j - 1], w2_r.at[j - 1], {"row": (r + j) % nr})
+        copy.start()
+        w2.append(copy)
+
+    f_copies[nq - 1].wait_recv()
+    z_copies = []
+    for j in range(1, nr + 1):
+        k = (r + j) % nr
+        cols = rows(k)
+        part = qt[:, cols] + jnp.dot(
+            gbuf[nq - 1, 1], a_ref[a_rows(nq - 1, 1), cols], preferred_element_type=F32
+        )
+        if j < nr:
+            z_out[j - 1] = part.astype(BF16)
+            copy = remote(z_out.at[j - 1], z_in.at[j - 1], z_s.at[j - 1], z_r.at[j - 1], {"row": k})
+            copy.start()
+            z_copies.append(copy)
+        else:
+            pf[0] = part
+
+    for copy in w2:
+        copy.wait_recv()
+    term = lambda i: jnp.where(
+        i == r, own_gw, gw_row[jnp.maximum((r + nr - i) % nr, 1) - 1]
+    )
+    full = term(0)
+    for i in range(1, nr):
+        full = full + term(i)
+    mine = pl.ds(pl.multiple_of(c * wr, wr), wr)
+    gw_all[mine, :] = full
+    w3 = []
+    for j in range(1, nc):
+        copy = remote(
+            gw_all.at[mine, :], gw_all.at[mine, :], w3_s.at[j - 1], w3_r.at[j - 1], {"col": (c + j) % nc}
+        )
+        copy.start()
+        w3.append(copy)
+
+    grad = pf[0]
+    for j in order:
+        z_copies[j - 1].wait_recv()
+        grad = grad + z_in[j - 1].astype(F32)
+    gf_ref[...] = jnp.transpose(grad).astype(BF16)
+    for copy in w3:
+        copy.wait_recv()
+    gw_ref[...] = gw_all[...]
+    for copy in x_copies + sib_copies + chip_copies + g_copies + f_copies + w1 + w2 + z_copies + w3:
+        copy.wait_send()
+
+
+def dense_device(features, weight, cotangent, blk_vals, blk_rows, blk_cols, blk_count):
+    nr, nc = lax.axis_size("row"), lax.axis_size("col")
+    nq = nc // 2
+    rd, width = cotangent.shape
+    side = blk_vals.shape[-1]
+    rb, cb = rd * nc // side, rd * nr // side
+    panel = densify(blk_vals[0, 0], blk_rows[0, 0], blk_cols[0, 0], blk_count[0], rb, cb)
+    vmem = pl.BlockSpec(memory_space=pltpu.VMEM)
+    dma = pltpu.SemaphoreType.DMA
+    wr = width // nc
+    activated, grad_weight, grad_features = pl.pallas_call(
+        functools.partial(layer_kernel, nr, nc),
+        out_shape=(
+            jax.ShapeDtypeStruct((rd, width), BF16),
+            jax.ShapeDtypeStruct((width, width), F32),
+            jax.ShapeDtypeStruct((rd, width), BF16),
+        ),
+        in_specs=[vmem, vmem, vmem, pl.BlockSpec(memory_space=pl.ANY)],
+        out_specs=(vmem, vmem, vmem),
+        scratch_shapes=[
+            pltpu.VMEM((rd * nc, rd * nr), BF16),
+            pltpu.VMEM((nr - 1, rd, width), BF16),
+            pltpu.VMEM((nc, rd, width), F32),
+            pltpu.VMEM((nq, rd, width), BF16),
+            pltpu.VMEM((nq, rd, width), BF16),
+            pltpu.VMEM((nq - 1, rd, width), BF16),
+            pltpu.VMEM((nq - 1, rd, width), BF16),
+            pltpu.VMEM((nq, 2, width, rd), BF16),
+            pltpu.VMEM((width, rd * nr), F32),
+            pltpu.VMEM((nr - 1, width, rd), BF16),
+            pltpu.VMEM((nr - 1, width, rd), BF16),
+            pltpu.VMEM((width, width), F32),
+            pltpu.VMEM((nc - 1, wr, width), F32),
+            pltpu.VMEM((wr, width), F32),
+            pltpu.VMEM((nr - 1, wr, width), F32),
+            pltpu.VMEM((width, width), F32),
+            dma(()),
+            dma((nr - 1,)), dma((nr - 1,)),
+            dma((nq,)), dma((nq,)),
+            dma((nq - 1,)), dma((nq - 1,)),
+            dma((nq - 1,)), dma((nq - 1,)),
+            dma((nq,)), dma((nq,)),
+            dma((nr - 1,)), dma((nr - 1,)),
+            dma((nc - 1,)), dma((nc - 1,)),
+            dma((nr - 1,)), dma((nr - 1,)),
+            dma((nc - 1,)), dma((nc - 1,)),
+        ],
+        compiler_params=pltpu.CompilerParams(collective_id=0, has_side_effects=True),
+        name="layer",
+    )(features[0], weight, cotangent, panel)
+    return activated, grad_weight, grad_features[None]
+
+
+def per_device(*arrays):
+    blk_vals, cotangent = arrays[3], arrays[2]
+    rd = cotangent.shape[0]
+    panel_bytes = rd * lax.axis_size("col") * rd * lax.axis_size("row") * 4
+    if panel_bytes <= DENSE_LIMIT:
+        return dense_device(*arrays)
+    return blockwise_device(*arrays)
+
+
 def solution(mesh):
     return jax.shard_map(
         per_device,

time: 425 us -> 71.8 us (0.17)
  waiting for transfers between devices: 214 us -> 0 us
  other arithmetic: 78.1 us -> 0 us
  Pallas kernels: 0 us -> 64.9 us
  matrix products: 47.9 us -> 0 us
  local copies, waits for them, and re-layouts: 52.5 us -> 4.8 us
  blocking collectives: 17.6 us -> 0 us
  between operations: 13.9 us -> 1.29 us
    psum x1 -> x0, waiting for transfers between devices: 129 us -> none  [per_device(): grad_weight = lax.psum(local_weight, ('row', 'col'))]
    scatter-add x2 -> x0, other arithmetic: 72.1 us -> none  [the longest x1 36.1 us: per_device(): jax.ops.segment_sum(products, row_ids, num_segments=row_blocks)]
    reduce_scatter x2 -> x0, waiting for transfers between devices: 69.4 us -> none  [the longest x1 43 us: per_device(): lax.psum_scatter(partial_rows.reshape(row_blocks * side, width), 'col', s...]
    pallas_call x0 -> x2, Pallas kernels: none -> 64.9 us  [the longest x1 55.3 us: dense_device(): pl.pallas_call(functools.partial(layer_kernel, nr, nc), out_shape=(jax.Sh...]
    dot_general x9 -> x0, matrix products: 47.9 us -> none  [the longest x6 44.3 us: one_group(): jnp.einsum(form, block_vals, picked, preferred_element_type=jnp.float32)]
    another operation x2 -> x0, local copies, waits for them, and re-layouts: 23 us -> none
    all_gather x1 -> x0, blocking collectives: 17.6 us -> none  [per_device(): panel = lax.all_gather(features, 'row', axis=1, tiled=True)]
    gather x6 -> x0, local copies, waits for them, and re-layouts: 16.7 us -> none  [one_group(): picked = jnp.take(source, block_ids, axis=0)]
  transfers between devices with their start and end apart: 4 -> 0, of which waited for: 4 -> 0; matrix products, arithmetic and copies ran while one was open for 3% -> 0% of each run, Pallas kernels for 0% -> 0%
where the time goes in v1:
time: 71.8 us; the launch traced here: 70.9 us
  Pallas kernels  64.9 us (90%)
  local copies, waits for them, and re-layouts  4.8 us (7%)
  between operations  1.29 us (2%)
    pallas_call x1, Pallas kernels, dense_device(): pl.pallas_call(functools.partial(layer_kernel, nr, nc), out_shape=(jax.Sh...  55.3 us
    pallas_call x1, Pallas kernels, densify(): pl.pallas_call(functools.partial(densify_kernel, cb), out_shape=jax.Shape...  9.56 us
    unnamed x3, local copies, waits for them, and re-layouts  4.8 us

profile of v1, /device:TPU:0, one launch (start us, length us, event | category | flops | bytes accessed | tf_op | source)
XLA Modules:
  0.0 70.9 jit_solution(7882867656456554835)
XLA Ops:
  1.3 9.6 %densify.1.a_hbm = bf16[2048,1024]{1,0:T(8,128)(2,1)} custom-call(s32[192]{0:T(256)} %bitcast.10, s32[192]{0:T(256)} %bitcast.11, s32[1]{0:T(128)} %bitcast.6.count_ref, bf16[192,128,128]{2,1,0:T(8,128)(2,1)} %bitcast.7), custom_call_target="tpu_custom_call" | custom-call | tf_op jit(solution)/shard_map/densify/pallas_call | solution.py:122
  10.8 55.3 %layer.1 = (bf16[256,256]{1,0:T(8,128)(2,1)}, f32[256,256]{1,0:T(8,128)}, bf16[256,256]{1,0:T(8,128)(2,1)}) custom-call(bf16[256,256]{1,0:T(8,128)(2,1)} %bitcast.8, bf16[256,256]{1,0:T(8,128)(2,1)} %w_ref.1, bf16[256,256]{1,0:T(8,128)(2,1)} %ct_ref.1, bf16[2048,1024]{1,0:T(8,128)(2,1)} %densify.1.a_hbm), custom_call_target="tpu_custom_call" | custom-call | tf_op jit(solution)/shard_map/layer/pallas_call | solution.py:338
  66.1 1.6 %copy.14 = bf16[256,256]{1,0:T(8,128)(2,1)} copy(bf16[256,256]{1,0:T(8,128)(2,1)} %get-tuple-element.12) | data formatting | bytes 262144
  67.7 1.7 %copy.15 = f32[256,256]{1,0:T(8,128)} copy(f32[256,256]{1,0:T(8,128)} %get-tuple-element.13) | data formatting | bytes 524288
  69.4 1.6 %copy.16 = bf16[1,256,256]{2,1,0:T(8,128)(2,1)} copy(bf16[1,256,256]{2,1,0:T(8,128)(2,1)} %bitcast.9) | data formatting | bytes 262144
